TPU v7x, 32 devices: a whole 2x2x4 slice. The times are simulated.
32 devices in a mesh: dp: 8 (over y, x, core), shard: 4 (over z).
Axes of the slice: x: 2, y: 2, z: 4, core: 2. Of those that a mesh axis runs over, the one named last changes fastest.
Arguments:
- activations: bfloat16 [4096, 4096], P('dp', 'shard'), may hold values from -6 to 6
- out_grads: bfloat16 [4096, 14336], P('dp', 'shard'), may hold values from -6 to 6
- sign_bits: int32 [14336], P('shard'), may hold values from 0 to 1
- block_ids: int32 [4, 8], replicated, may hold values from 0 to 111, as said below
Outputs:
- gram: float32 [4096, 1024], P('shard')
Inputs may be any that keep to these rules, and one draw needn't show every extreme that they name: `block_ids`: row o holds 4 runs of 2 entries; the entries of a run are distinct blocks of one shard s (ids s * 28 + 0 to s * 28 + 27), and the runs of a row come from distinct shards.
All inputs are finite; a program needn't handle non-finite values.
Results may differ from a plain program's by a relative error of at most 0.006.
Values may be sent and summed in bfloat16 or wider, within the bound.
A program may use at most 64 MiB of HBM per device.

v0:
```python
import math
import jax
import jax.numpy as jnp
from jax import lax
from jax.sharding import PartitionSpec as P

BLK = 128
CAP = 2


def partner_2(x, axis, distance):
    return lax.ppermute(x, axis, [(i, i ^ 1 << distance) for i in range(lax.axis_size(axis))])


def parity_table(count):
    index = jnp.arange(count, dtype=jnp.int32)
    total = jnp.zeros((count, count), jnp.int32)
    for level in range(count.bit_length() - 1):
        total = total + (
            jnp.right_shift(index[:, None], level) & jnp.right_shift(index[None, :], level) & 1
        )
    return (1 - 2 * (total % 2)).astype(jnp.float32)


def route_sampled(mixed, block_ids, me_index, shards, blocks_per, tokens, width):
    groups = block_ids.shape[1] // CAP
    sources = block_ids[:, ::CAP] // blocks_per
    local_ids = (block_ids % blocks_per).reshape(shards, groups, CAP)
    matched = sources == me_index
    chosen = jnp.sum(jnp.where(matched[:, :, None], local_ids, 0), axis=1)
    live_rows = jnp.any(matched, axis=1).astype(jnp.bfloat16)
    outgoing = jnp.take(mixed, chosen.reshape(-1), axis=0).reshape(shards, CAP, tokens, width)
    return (outgoing * live_rows[:, None, None, None], jnp.take(sources, me_index, axis=0))


def body(activations, out_grads, sign_bits, block_ids):
    shards = lax.axis_size("shard")
    me_index = lax.axis_index("shard")
    tokens = out_grads.shape[0]
    width = BLK
    own_blocks = block_ids.shape[1]
    blocks_per = out_grads.shape[1] // width
    model_width = activations.shape[1] * shards
    inv_block = 1.0 / math.sqrt(width)
    inv_shard = 1.0 / math.sqrt(shards)
    partial_gram = jnp.dot(activations, activations.T, preferred_element_type=jnp.float32)
    token_gram = lax.psum(partial_gram, "shard").astype(jnp.bfloat16)
    sign_values = (1 - 2 * sign_bits).astype(jnp.bfloat16)
    flipped = (out_grads * sign_values[None, :]).reshape(tokens, blocks_per, width)
    block_table = parity_table(width).astype(jnp.bfloat16)
    local_mix = jnp.einsum("tbj,jk->btk", flipped, block_table, preferred_element_type=jnp.float32)
    local_mix = (local_mix * inv_block).astype(jnp.bfloat16)
    running = local_mix.astype(jnp.float32)
    for level in range(shards.bit_length() - 1):
        partner = partner_2(running, "shard", level)
        upper = jnp.right_shift(me_index, level) & 1 == 1
        running = jnp.where(upper, partner - running, running + partner)
    mixed = (running * inv_shard).astype(jnp.bfloat16)
    outgoing, own_sources = route_sampled(
        mixed, block_ids, me_index, shards, blocks_per, tokens, width
    )
    incoming = lax.all_to_all(outgoing, "shard", split_axis=0, concat_axis=0, tiled=True)
    sketched = jnp.take(incoming, own_sources, axis=0).reshape(own_blocks, tokens, width)
    weighted = jnp.einsum(
        "tu,jub->jtb", token_gram, sketched, preferred_element_type=jnp.float32
    ).astype(jnp.bfloat16)
    block_gram = jnp.einsum("jtb,ktc->jbkc", sketched, weighted, preferred_element_type=jnp.float32)
    own_cols = own_blocks * width
    block_gram = block_gram.reshape(own_cols, own_cols)
    summed = lax.psum(block_gram, "dp")
    return summed / (lax.axis_size("dp") * tokens * model_width)


def solution(mesh):
    in_specs = (P("dp", "shard"), P("dp", "shard"), P("shard"), P())
    out_specs = P("shard", None)
    return jax.shard_map(body, mesh=mesh, in_specs=in_specs, out_specs=out_specs, check_vma=False)
```

profile of v0, /device:TPU:0, one launch (start us, length us, event | category | flops | bytes accessed | tf_op | source)
XLA Modules:
  0.0 690.9 jit_solution(8151458818415333310)
XLA Ops:
  6.6 6.0 copy.15
  12.6 0.0 copy-done.1
  12.6 3.3 broadcast_multiply_fusion.1
  15.9 4.3 convert_bitcast_fusion
  20.2 3.1 collective-permute-start
  23.3 158.3 %collective-permute-done = f32[28,512,128]{1,2,0:T(8,128)} collective-permute-done((f32[28,512,128]{1,2,0:T(8,128)}, f32[28,512,128]{1,2,0:T(8,128)}, u32[]{:S(2)}, u32[]{:S(2)}) %collective-permute-start) | collective-permute-done | bytes 7340064 | tf_op jit(solution)/shard_map/ppermute | solution.py:12
  181.6 10.6 %add_select_fusion = f32[28,512,128]{1,2,0:T(8,128)} fusion(f32[28,512,128]{1,2,0:T(8,128)} %convert_bitcast_fusion, f32[28,512,128]{1,2,0:T(8,128)} %collective-permute-done, pred[]{:T(512)S(6)} %eq.19), kind=kLoop, calls=%fused_computation.4 | loop fusion | flops 5505024 | bytes 22020096 | tf_op jit(solution)/shard_map/jit(_where)/select_n | solution.py:57
  192.1 2.8 collective-permute-start.1
  194.9 0.1 slice.3
  195.0 0.1 copy.13
  195.1 0.1 fusion.32
  195.2 0.1 copy.12
  195.3 0.1 copy.17
  195.4 0.1 reshape.154
  195.5 0.1 copy.14
  195.7 0.1 broadcast_in_dim.63
  195.7 0.1 broadcast_in_dim.64
  195.8 314.0 %collective-permute-done.1 = f32[28,512,128]{1,2,0:T(8,128)} collective-permute-done((f32[28,512,128]{1,2,0:T(8,128)}, f32[28,512,128]{1,2,0:T(8,128)}, u32[]{:S(2)}, u32[]{:S(2)}) %collective-permute-start.1) | collective-permute-done | bytes 7340064 | tf_op jit(solution)/shard_map/ppermute | solution.py:12
  509.8 9.1 %multiply_convert_fusion = bf16[28,512,128]{1,2,0:T(8,128)(2,1)} fusion(f32[28,512,128]{1,2,0:T(8,128)} %add_select_fusion, f32[28,512,128]{1,2,0:T(8,128)} %collective-permute-done.1, pred[]{:T(512)S(6)} %eq.18), kind=kLoop, calls=%fused_computation.3 | loop fusion | flops 9175040 | bytes 18350080 | tf_op jit(solution)/shard_map/convert_element_type | solution.py:58
  518.9 2.6 gather_fusion
  521.5 1.1 select_multiply_fusion
  522.7 4.6 all-to-all-start
  527.3 0.7 fusion.33
  528.1 63.9 %all-reduce.4 = bf16[512,512]{1,0:T(8,128)(2,1)} all-reduce(f32[512,512]{1,0:T(8,128)S(1)} %fusion.33), channel_id=1, replica_groups=mesh['dp'=8,'shard'=4] {'shard'}, use_global_device_ids=true, to_apply=%region_2.3 | all-reduce | flops 262144 | bytes 1572864 | tf_op jit(solution)/shard_map/psum | solution.py:47
  591.9 0.0 all-to-all-done
  591.9 0.6 gather_fusion.1
  592.6 0.2 bitcast_select_fusion
  592.7 1.8 convolution_convert_fusion
  594.5 3.3 fusion.34
  597.8 0.0 all-reduce.3.cloned.1.call-update
  597.8 81.2 %all-reduce.3.cloned.1.call-done = f32[1024,1024]{1,0:T(8,128)} async-done(((f32[1024,1024]{1,0:T(8,128)}), f32[1024,1024]{1,0:T(8,128)}) %all-reduce.3.cloned.1.call-update) | async-done | bytes 4194320 | tf_op jit(solution)/shard_map/psum | solution.py:70
  679.0 5.0 broadcast_multiply_fusion
  (20 shorter events, 0.1 us)
Async XLA Ops:
  6.5 520.8 %copy-start = (bf16[512,1024]{1,0:T(8,128)(2,1)S(1)}, bf16[512,1024]{1,0:T(8,128)(2,1)}, u32[]{:S(2)}) copy-start(bf16[512,1024]{1,0:T(8,128)(2,1)} %param.4) | copy-start | bytes 3145732
  6.5 6.0 copy-start.1
  20.2 161.4 %collective-permute-start = (f32[28,512,128]{1,2,0:T(8,128)}, f32[28,512,128]{1,2,0:T(8,128)}, u32[]{:S(2)}, u32[]{:S(2)}) collective-permute-start(f32[28,512,128]{1,2,0:T(8,128)} %convert_bitcast_fusion), channel_id=1, source_target_pairs={{0,1},{1,0},{2,3},{3,2},{4,5},{5,4},{6,7},{7,6},{8,9},{9,8},{10,11... | collective-permute-start | bytes 22020104 | tf_op jit(solution)/shard_map/ppermute | solution.py:12
  23.3 171.6 %copy-start.2 = (s32[4,8]{1,0:T(4,128)S(1)}, s32[4,8]{1,0:T(4,128)}, u32[]{:S(2)}) copy-start(s32[4,8]{1,0:T(4,128)} %param.7) | copy-start | bytes 388
  192.1 317.7 %collective-permute-start.1 = (f32[28,512,128]{1,2,0:T(8,128)}, f32[28,512,128]{1,2,0:T(8,128)}, u32[]{:S(2)}, u32[]{:S(2)}) collective-permute-start(f32[28,512,128]{1,2,0:T(8,128)} %add_select_fusion), channel_id=1, source_target_pairs={{0,2},{1,3},{2,0},{3,1},{4,6},{5,7},{6,4},{7,5},{8,10},{9,11},{10,... | collective-permute-start | bytes 22020104 | tf_op jit(solution)/shard_map/ppermute | solution.py:12
  522.7 69.3 %all-to-all-start = ((bf16[4,2,512,128]{2,3,1,0:T(8,128)(2,1)}), bf16[4,2,512,128]{2,3,1,0:T(8,128)(2,1)S(1)}, u32[]{:S(2)}, u32[]{:S(2)}) async-start(bf16[4,2,512,128]{2,3,1,0:T(8,128)(2,1)} %select_multiply_fusion), calls=%async_computation | async-start | bytes 2097152 | tf_op jit(solution)/shard_map/all_to_all | solution.py:62
  527.3 151.7 %all-reduce.3.cloned.1.call-start = ((), (), s32[]{:S(2)}) async-start(), calls=%async_computation.1 | async-start | bytes 8388608 | tf_op jit(solution)/shard_map/psum | solution.py:70
Sparse Core Ops, SparseCore 0:
  598.0 80.9 all-reduce.2
where the time goes:
time: 691 us
  waiting for transfers between devices  553 us (80%)
  blocking collectives  63.9 us (9%)
  other arithmetic  29.5 us (4%)
  between operations  13.5 us (2%)
  starting transfers between devices  10.5 us (2%)
  matrix products  10.1 us (1%)
  local copies, waits for them, and re-layouts  10 us (1%)
    ppermute x2, waiting for transfers between devices, partner_2(): lax.ppermute(x, axis, [(i, i ^ 1 << distance) for i in range(lax.axis_siz...  472 us
    psum x1, waiting for transfers between devices, body(): summed = lax.psum(block_gram, 'dp')  81.2 us
    psum x1, blocking collectives, body(): token_gram = lax.psum(partial_gram, 'shard').astype(jnp.bfloat16)  63.9 us
  transfers between devices with their start and end apart: 4, of which 3 were waited for; matrix products, arithmetic and copies ran while one was open for 0% of the time, Pallas kernels for 0%

commit v1 on v0

--- a/solution.py
+++ b/solution.py
@@ -67,7 +67,9 @@
     block_gram = jnp.einsum("jtb,ktc->jbkc", sketched, weighted, preferred_element_type=jnp.float32)
     own_cols = own_blocks * width
     block_gram = block_gram.reshape(own_cols, own_cols)
-    summed = lax.psum(block_gram, "dp")
+    summed = block_gram
+    for hop in (1, 2, 4):
+        summed = summed + lax.ppermute(summed, "dp", [(dev, dev ^ hop) for dev in range(8)])
     return summed / (lax.axis_size("dp") * tokens * model_width)
 
 

time: 691 us -> 787 us (1.14)
  waiting for transfers between devices: 553 us -> 661 us
  between operations: 13.5 us -> 0.14 us
    ppermute x0 -> x3, waiting for transfers between devices: none -> 189 us  [body(): lax.ppermute(summed, 'dp', [(dev, dev ^ hop) for dev in range(8)])]
    psum x1 -> x0, waiting for transfers between devices: 81.2 us -> none  [body(): summed = lax.psum(block_gram, 'dp')]
  transfers between devices with their start and end apart: 4 -> 6, of which waited for: 3 -> 5; matrix products, arithmetic and copies ran while one was open for 0% -> 0% of each run, Pallas kernels for 0% -> 0%
where the time goes in v1:
time: 787 us
  waiting for transfers between devices  661 us (84%)
  blocking collectives  63.8 us (8%)
  other arithmetic  30.2 us (4%)
  starting transfers between devices  13.6 us (2%)
  local copies, waits for them, and re-layouts  10 us (1%)
  matrix products  8.07 us (1%)
    ppermute x2, waiting for transfers between devices, partner_2(): lax.ppermute(x, axis, [(i, i ^ 1 << distance) for i in range(lax.axis_siz...  472 us
    ppermute x3, waiting for transfers between devices, body(): lax.ppermute(summed, 'dp', [(dev, dev ^ hop) for dev in range(8)])  189 us
    psum x1, blocking collectives, body(): token_gram = lax.psum(partial_gram, 'shard').astype(jnp.bfloat16)  63.8 us
  transfers between devices with their start and end apart: 6, of which 5 were waited for; matrix products, arithmetic and copies ran while one was open for 0% of the time, Pallas kernels for 0%

profile of v1, /device:TPU:0, one launch (start us, length us, event | category | flops | bytes accessed | tf_op | source)
XLA Modules:
  0.0 786.7 jit_solution(17703151579495159882)
XLA Ops:
  0.0 6.0 copy.15
  6.1 3.3 broadcast_multiply_fusion
  9.4 4.3 convert_bitcast_fusion
  13.7 3.1 collective-permute-start
  16.7 158.3 %collective-permute-done = f32[28,512,128]{1,2,0:T(8,128)} collective-permute-done((f32[28,512,128]{1,2,0:T(8,128)}, f32[28,512,128]{1,2,0:T(8,128)}, u32[]{:S(2)}, u32[]{:S(2)}) %collective-permute-start) | collective-permute-done | bytes 7340064 | tf_op jit(solution)/shard_map/ppermute | solution.py:12
  175.0 10.6 %add_select_fusion = f32[28,512,128]{1,2,0:T(8,128)} fusion(f32[28,512,128]{1,2,0:T(8,128)} %convert_bitcast_fusion, f32[28,512,128]{1,2,0:T(8,128)} %collective-permute-done, pred[]{:T(512)S(6)} %eq.19), kind=kLoop, calls=%fused_computation.4 | loop fusion | flops 5505024 | bytes 22020096 | tf_op jit(solution)/shard_map/jit(_where)/select_n | solution.py:57
  185.6 2.8 collective-permute-start.1
  188.4 0.1 slice.3
  188.5 0.1 fusion.32
  188.7 0.1 copy.12
  188.8 0.1 copy.17
  189.0 0.1 copy.14
  189.2 0.1 broadcast_in_dim.64
  189.3 313.9 %collective-permute-done.1 = f32[28,512,128]{1,2,0:T(8,128)} collective-permute-done((f32[28,512,128]{1,2,0:T(8,128)}, f32[28,512,128]{1,2,0:T(8,128)}, u32[]{:S(2)}, u32[]{:S(2)}) %collective-permute-start.1) | collective-permute-done | bytes 7340064 | tf_op jit(solution)/shard_map/ppermute | solution.py:12
  503.3 9.1 %multiply_convert_fusion = bf16[28,512,128]{1,2,0:T(8,128)(2,1)} fusion(f32[28,512,128]{1,2,0:T(8,128)} %add_select_fusion, f32[28,512,128]{1,2,0:T(8,128)} %collective-permute-done.1, pred[]{:T(512)S(6)} %eq.18), kind=kLoop, calls=%fused_computation.3 | loop fusion | flops 9175040 | bytes 18350080 | tf_op jit(solution)/shard_map/convert_element_type | solution.py:58
  512.3 2.6 gather_fusion
  515.0 1.1 select_multiply_fusion
  516.1 4.7 all-to-all-start
  520.8 0.7 fusion.33
  521.6 63.8 %all-reduce.1 = bf16[512,512]{1,0:T(8,128)(2,1)} all-reduce(f32[512,512]{1,0:T(8,128)S(1)} %fusion.33), channel_id=1, replica_groups=mesh['dp'=8,'shard'=4] {'shard'}, use_global_device_ids=true, to_apply=%region_2.3 | all-reduce | flops 262144 | bytes 1572864 | tf_op jit(solution)/shard_map/psum | solution.py:47
  585.4 0.6 gather_fusion.1
  586.0 0.2 bitcast_select_fusion
  586.2 1.8 convolution_convert_fusion
  588.0 1.3 fusion.34
  589.4 7.1 collective-permute-done.2
  596.5 1.4 add.98
  597.9 1.5 collective-permute-start.3
  599.4 91.2 %collective-permute-done.3 = f32[1024,1024]{1,0:T(8,128)S(1)} collective-permute-done((f32[1024,1024]{1,0:T(8,128)S(1)}, f32[1024,1024]{1,0:T(8,128)S(1)}, u32[]{:S(2)}, u32[]{:S(2)}) %collective-permute-start.3) | collective-permute-done | bytes 4194336 | tf_op jit(solution)/shard_map/ppermute | solution.py:72
  690.5 1.4 add.99
  691.9 1.6 collective-permute-start.4
  693.5 90.3 %collective-permute-done.4 = f32[1024,1024]{1,0:T(8,128)S(1)} collective-permute-done((f32[1024,1024]{1,0:T(8,128)S(1)}, f32[1024,1024]{1,0:T(8,128)S(1)}, u32[]{:S(2)}, u32[]{:S(2)}) %collective-permute-start.4) | collective-permute-done | bytes 4194336 | tf_op jit(solution)/shard_map/ppermute | solution.py:72
  783.7 3.0 add_multiply_fusion
  (25 shorter events, 0.4 us)
Async XLA Ops:
  0.0 520.8 %copy-start = (bf16[512,1024]{1,0:T(8,128)(2,1)S(1)}, bf16[512,1024]{1,0:T(8,128)(2,1)}, u32[]{:S(2)}) copy-start(bf16[512,1024]{1,0:T(8,128)(2,1)} %param.4) | copy-start | bytes 3145732
  0.0 6.0 copy-start.1
  13.7 161.4 %collective-permute-start = (f32[28,512,128]{1,2,0:T(8,128)}, f32[28,512,128]{1,2,0:T(8,128)}, u32[]{:S(2)}, u32[]{:S(2)}) collective-permute-start(f32[28,512,128]{1,2,0:T(8,128)} %convert_bitcast_fusion), channel_id=1, source_target_pairs={{0,1},{1,0},{2,3},{3,2},{4,5},{5,4},{6,7},{7,6},{8,9},{9,8},{10,11... | collective-permute-start | bytes 22020104 | tf_op jit(solution)/shard_map/ppermute | solution.py:12
  16.7 171.6 %copy-start.2 = (s32[4,8]{1,0:T(4,128)S(1)}, s32[4,8]{1,0:T(4,128)}, u32[]{:S(2)}) copy-start(s32[4,8]{1,0:T(4,128)} %param.7) | copy-start | bytes 388
  185.6 317.7 %collective-permute-start.1 = (f32[28,512,128]{1,2,0:T(8,128)}, f32[28,512,128]{1,2,0:T(8,128)}, u32[]{:S(2)}, u32[]{:S(2)}) collective-permute-start(f32[28,512,128]{1,2,0:T(8,128)} %add_select_fusion), channel_id=1, source_target_pairs={{0,2},{1,3},{2,0},{3,1},{4,6},{5,7},{6,4},{7,5},{8,10},{9,11},{10,... | collective-permute-start | bytes 22020104 | tf_op jit(solution)/shard_map/ppermute | solution.py:12
  516.1 69.3 %all-to-all-start = ((bf16[4,2,512,128]{2,3,1,0:T(8,128)(2,1)}), bf16[4,2,512,128]{2,3,1,0:T(8,128)(2,1)S(1)}, u32[]{:S(2)}, u32[]{:S(2)}) async-start(bf16[4,2,512,128]{2,3,1,0:T(8,128)(2,1)} %select_multiply_fusion), calls=%async_computation | async-start | bytes 2097152 | tf_op jit(solution)/shard_map/all_to_all | solution.py:62
  589.3 7.2 collective-permute-start.2
  597.9 92.7 %collective-permute-start.3 = (f32[1024,1024]{1,0:T(8,128)S(1)}, f32[1024,1024]{1,0:T(8,128)S(1)}, u32[]{:S(2)}, u32[]{:S(2)}) collective-permute-start(f32[1024,1024]{1,0:T(8,128)S(1)} %add.98), channel_id=1, source_target_pairs={{0,8},{4,12},{8,0},{12,4},{16,24},{20,28},{24,16},{28,20},{1,9},{5... | collective-permute-start | bytes 12582920 | tf_op jit(solution)/shard_map/ppermute | solution.py:72
  691.9 91.8 %collective-permute-start.4 = (f32[1024,1024]{1,0:T(8,128)S(1)}, f32[1024,1024]{1,0:T(8,128)S(1)}, u32[]{:S(2)}, u32[]{:S(2)}) collective-permute-start(f32[1024,1024]{1,0:T(8,128)S(1)} %add.99), channel_id=1, source_target_pairs={{0,16},{4,20},{8,24},{12,28},{16,0},{20,4},{24,8},{28,12},{1,17},{... | collective-permute-start | bytes 12582920 | tf_op jit(solution)/shard_map/ppermute | solution.py:72
